TPU v7x, 32 devices: a whole 2x2x4 slice. The times are simulated.
32 devices in a mesh: dp: 16 (over z, y, core), mp: 2 (over x).
Axes of the slice: x: 2, y: 2, z: 4, core: 2. Of those that a mesh axis runs over, the one named last changes fastest.
Arguments:
- inputs: bfloat16 [64, 320, 1024], P('dp', 'mp'), may hold values from -6 to 6
- teacher: bfloat16 [64, 320, 1024], P('dp', 'mp'), may hold values from -6 to 6
- keep_mask: int32 [64, 320], P('dp'), may hold values from 0 to 1, as said below
- gain_attn: bfloat16 [1024], P('dp'), may hold values from 0.099609375 to 1.8984375
- qkv_weight: bfloat16 [1024, 3, 1024], P('dp', None, 'mp'), may hold values from -0.25 to 0.25
- out_weight: bfloat16 [1024, 1024], P('dp', 'mp'), may hold values from -0.5 to 0.5
- gain_mlp: bfloat16 [1024], P('dp'), may hold values from 0.099609375 to 1.8984375
- up_weight: bfloat16 [1024, 4096], P('dp', 'mp'), may hold values from -0.1875 to 0.1875
- down_weight: bfloat16 [1024, 4096], P('dp', 'mp'), may hold values from -0.125 to 0.125
Outputs:
- output: bfloat16 [64, 320, 1024], P('dp', 'mp')
- loss: float32 [], replicated
- input_grad: float32 [64, 320, 1024], P('dp', 'mp')
- gain_attn_grad: float32 [1024], P('dp')
- qkv_grad: float32 [1024, 3, 1024], P('dp', None, 'mp')
- out_grad: float32 [1024, 1024], P('dp', 'mp')
- gain_mlp_grad: float32 [1024], P('dp')
- up_grad: float32 [1024, 4096], P('dp', 'mp')
- down_grad: float32 [1024, 4096], P('dp', 'mp')
Inputs may be any that keep to these rules, and one draw needn't show every extreme that they name: `keep_mask`: the first 64 positions of every image are 1; how many of its other positions an image keeps varies from image to image and from draw to draw.
All inputs are finite; a program needn't handle non-finite values.
Results may differ from a plain program's by a relative error of at most 0.009.
The roundings to bfloat16 on the way count: a program that leaves them out, or rounds other values in their place, can miss the bound.
Values may be sent and summed in bfloat16 or wider, within the bound.
A program may use at most 96 MiB of HBM per device.

v0:
```python
import jax
import jax.numpy as jnp
from jax import lax
from jax.sharding import PartitionSpec as P

HDIM = 64
MICRO = 2
norm_epsilon = 1e-06


def normalize(values):
    centre = values - jnp.mean(values, axis=-1, keepdims=True)
    spread = jnp.mean(centre * centre, axis=-1, keepdims=True)
    scaled = lax.rsqrt(spread + norm_epsilon)
    return (centre * scaled, scaled)


def norm_back(grad_out, unit_rows, scaled, gain_values):
    grad_scaled = grad_out * gain_values
    first = jnp.mean(grad_scaled, axis=-1, keepdims=True)
    second = jnp.mean(grad_scaled * unit_rows, axis=-1, keepdims=True)
    return scaled * (grad_scaled - first - unit_rows * second)


def exact_gelu(values):
    return jax.nn.gelu(values, approximate=False)


def full_rows(piece):
    return lax.all_gather(piece, "mp", axis=1, tiled=True)


def row_sums(partial_rows):
    return lax.psum_scatter(partial_rows, "mp", scatter_dimension=1, tiled=True)


def full_grads(piece):
    return lax.all_gather(piece, "mp", axis=1, tiled=True)


def sum_grads(partial_rows):
    return lax.psum_scatter(partial_rows, "mp", scatter_dimension=1, tiled=True)


def split_heads(projected):
    image_count, seq_length = (projected.shape[0], projected.shape[1])
    head_count = projected.shape[3] // HDIM
    queries = projected[:, :, 0].reshape(image_count, seq_length, head_count, HDIM)
    key_rows = projected[:, :, 1].reshape(image_count, seq_length, head_count, HDIM)
    value_rows = projected[:, :, 2].reshape(image_count, seq_length, head_count, HDIM)
    return (queries, key_rows, value_rows)


def masked_scores(queries, key_rows, allowed):
    scores = jnp.einsum(
        "bqhe,bkhe->bhqk", queries, key_rows, preferred_element_type=jnp.float32
    ) * HDIM ** (-0.5)
    return jnp.where(allowed, scores, -1e30)


def attend(projected, allowed):
    queries, key_rows, value_rows = split_heads(projected)
    scores = masked_scores(queries, key_rows, allowed)
    maximum = jnp.max(scores, axis=-1, keepdims=True)
    raised = jnp.exp(scores - maximum)
    normaliser = jnp.sum(raised, axis=-1, keepdims=True)
    weights_soft = (raised / normaliser).astype(jnp.bfloat16)
    log_total = maximum + jnp.log(normaliser)
    mixture = jnp.einsum(
        "bhqk,bkhe->bqhe", weights_soft, value_rows, preferred_element_type=jnp.float32
    )
    shaped = mixture.reshape(projected.shape[0], projected.shape[1], projected.shape[3])
    return (shaped.astype(jnp.bfloat16), log_total)


def attend_back(projected, allowed, log_total, grad_heads):
    queries, key_rows, value_rows = split_heads(projected)
    scores = masked_scores(queries, key_rows, allowed)
    weights_soft = jnp.exp(scores - log_total)
    grad_mix = grad_heads.reshape(queries.shape)
    grad_weights = jnp.einsum(
        "bqhe,bkhe->bhqk", grad_mix, value_rows, preferred_element_type=jnp.float32
    )
    inner = jnp.sum(grad_weights * weights_soft, axis=-1, keepdims=True)
    grad_scores = (weights_soft * (grad_weights - inner)).astype(jnp.bfloat16)
    grad_query = jnp.einsum(
        "bhqk,bkhe->bqhe", grad_scores, key_rows, preferred_element_type=jnp.float32
    ) * HDIM ** (-0.5)
    grad_key = jnp.einsum(
        "bhqk,bqhe->bkhe", grad_scores, queries, preferred_element_type=jnp.float32
    ) * HDIM ** (-0.5)
    grad_value = jnp.einsum(
        "bhqk,bqhe->bkhe",
        weights_soft.astype(jnp.bfloat16),
        grad_mix,
        preferred_element_type=jnp.float32,
    )
    stacked = jnp.stack(
        [
            grad_query.astype(jnp.bfloat16),
            grad_key.astype(jnp.bfloat16),
            grad_value.astype(jnp.bfloat16),
        ],
        axis=2,
    )
    return stacked.reshape(projected.shape)


def per_device(
    inputs, teacher, keep_mask, gain_attn, qkv_weight, out_weight, gain_mlp, up_weight, down_weight
):
    owned = (gain_attn, gain_mlp, qkv_weight, out_weight, up_weight, down_weight)
    half_len = inputs.shape[1]
    offset = lax.axis_index("mp") * half_len
    keep_local = lax.dynamic_slice_in_dim(keep_mask, offset, half_len, 1)
    valid_total = lax.psum(jnp.sum(keep_local).astype(jnp.float32), ("dp", "mp"))
    token_total = inputs.shape[0] * lax.axis_size("dp") * half_len * lax.axis_size("mp")
    loss_factor = 2.0 * token_total / valid_total
    per_micro = inputs.shape[0] // MICRO
    summed = tuple(
        (
            jnp.zeros((piece.shape[0] * lax.axis_size("dp"),) + piece.shape[1:], jnp.float32)
            for piece in owned
        )
    )
    outputs = []
    input_grads = []
    loss_local = jnp.zeros((), jnp.float32)
    for micro_step in range(MICRO):
        first_image = micro_step * per_micro
        field_in = inputs[first_image : first_image + per_micro].astype(jnp.float32)
        target = teacher[first_image : first_image + per_micro].astype(jnp.float32)
        keep_rows = keep_local[first_image : first_image + per_micro].astype(jnp.float32)[
            :, :, None
        ]
        allowed = (keep_mask[first_image : first_image + per_micro] > 0)[:, None, None, :]
        forward_set = (
            lax.all_gather(gain_attn, "dp", axis=0, tiled=True),
            lax.all_gather(gain_mlp, "dp", axis=0, tiled=True),
            lax.all_gather(qkv_weight, "dp", axis=0, tiled=True),
            lax.all_gather(out_weight, "dp", axis=0, tiled=True),
            lax.all_gather(up_weight, "dp", axis=0, tiled=True),
            lax.all_gather(down_weight, "dp", axis=0, tiled=True),
        )
        gain_one = forward_set[0].astype(jnp.float32)
        gain_two = forward_set[1].astype(jnp.float32)
        w_qkv, w_out, w_up, w_down = (
            forward_set[2],
            forward_set[3],
            forward_set[4],
            forward_set[5],
        )
        unit_one, scaled_one = normalize(field_in)
        normed_full = full_rows((unit_one * gain_one).astype(jnp.bfloat16))
        projected = jnp.einsum(
            "bsd,dcf->bscf", normed_full, w_qkv, preferred_element_type=jnp.float32
        ).astype(jnp.bfloat16)
        heads_out, log_total = attend(projected, allowed)
        attended = row_sums(
            jnp.einsum("bsf,df->bsd", heads_out, w_out, preferred_element_type=jnp.float32)
        )
        middle = field_in + attended
        unit_two, scaled_two = normalize(middle)
        normed_wide = full_rows((unit_two * gain_two).astype(jnp.bfloat16))
        hidden_in = jnp.einsum("bsd,df->bsf", normed_wide, w_up, preferred_element_type=jnp.float32)
        activated, gelu_back = jax.vjp(exact_gelu, hidden_in)
        hidden = activated.astype(jnp.bfloat16)
        branch = row_sums(
            jnp.einsum("bsf,df->bsd", hidden, w_down, preferred_element_type=jnp.float32)
        )
        result = middle + branch
        outputs.append((result * keep_rows).astype(jnp.bfloat16))
        error = result - target
        loss_local = loss_local + jnp.sum(
            keep_rows * jnp.mean(error * error, axis=-1, keepdims=True)
        )
        grad_result = loss_factor * keep_rows * error
        backward_set = (
            lax.all_gather(gain_attn, "dp", axis=0, tiled=True),
            lax.all_gather(gain_mlp, "dp", axis=0, tiled=True),
            lax.all_gather(qkv_weight, "dp", axis=0, tiled=True),
            lax.all_gather(out_weight, "dp", axis=0, tiled=True),
            lax.all_gather(up_weight, "dp", axis=0, tiled=True),
            lax.all_gather(down_weight, "dp", axis=0, tiled=True),
        )
        w_qkv, w_out, w_up, w_down = (
            backward_set[2],
            backward_set[3],
            backward_set[4],
            backward_set[5],
        )
        grad_branch = full_grads(grad_result.astype(jnp.bfloat16))
        grad_hidden = jnp.einsum(
            "bsd,df->bsf", grad_branch, w_down, preferred_element_type=jnp.float32
        )
        down_part = jnp.einsum(
            "bsd,bsf->df", grad_branch, hidden, preferred_element_type=jnp.float32
        )
        grad_pre = gelu_back(grad_hidden)[0].astype(jnp.bfloat16)
        up_part = jnp.einsum(
            "bsd,bsf->df", normed_wide, grad_pre, preferred_element_type=jnp.float32
        )
        grad_normed_two = sum_grads(
            jnp.einsum("bsf,df->bsd", grad_pre, w_up, preferred_element_type=jnp.float32)
        )
        gain_mlp_part = jnp.sum(grad_normed_two * unit_two, axis=(0, 1))
        grad_middle = grad_result + norm_back(grad_normed_two, unit_two, scaled_two, gain_two)
        grad_attended = full_grads(grad_middle.astype(jnp.bfloat16))
        grad_heads = jnp.einsum(
            "bsd,df->bsf", grad_attended, w_out, preferred_element_type=jnp.float32
        ).astype(jnp.bfloat16)
        out_part = jnp.einsum(
            "bsd,bsf->df", grad_attended, heads_out, preferred_element_type=jnp.float32
        )
        grad_projected = attend_back(projected, allowed, log_total, grad_heads)
        qkv_part = jnp.einsum(
            "bsd,bscf->dcf", normed_full, grad_projected, preferred_element_type=jnp.float32
        )
        grad_normed_one = sum_grads(
            jnp.einsum("bscf,dcf->bsd", grad_projected, w_qkv, preferred_element_type=jnp.float32)
        )
        gain_attn_part = jnp.sum(grad_normed_one * unit_one, axis=(0, 1))
        input_grads.append(grad_middle + norm_back(grad_normed_one, unit_one, scaled_one, gain_one))
        fresh = (gain_attn_part, gain_mlp_part, qkv_part, out_part, up_part, down_part)
        summed = tuple((current + added for current, added in zip(summed, fresh)))
    summed = (
        lax.psum_scatter(summed[0], "dp", scatter_dimension=0, tiled=True),
        lax.psum_scatter(summed[1], "dp", scatter_dimension=0, tiled=True),
        lax.psum_scatter(summed[2], "dp", scatter_dimension=0, tiled=True),
        lax.psum_scatter(summed[3], "dp", scatter_dimension=0, tiled=True),
        lax.psum_scatter(summed[4], "dp", scatter_dimension=0, tiled=True),
        lax.psum_scatter(summed[5], "dp", scatter_dimension=0, tiled=True),
    )
    gain_sums = lax.psum((summed[0], summed[1]), "mp")
    loss = lax.psum(loss_local, ("dp", "mp")) / valid_total
    output = jnp.concatenate(outputs, axis=0)
    input_grad = jnp.concatenate(input_grads, axis=0)
    return (
        output,
        loss,
        input_grad,
        gain_sums[0],
        summed[2],
        summed[3],
        gain_sums[1],
        summed[4],
        summed[5],
    )


def solution(mesh):
    in_specs = (
        P("dp", "mp", None),
        P("dp", "mp", None),
        P("dp", None),
        P("dp"),
        P("dp", None, "mp"),
        P("dp", "mp"),
        P("dp"),
        P("dp", "mp"),
        P("dp", "mp"),
    )
    out_specs = (
        P("dp", "mp", None),
        P(),
        P("dp", "mp", None),
        P("dp"),
        P("dp", None, "mp"),
        P("dp", "mp"),
        P("dp"),
        P("dp", "mp"),
        P("dp", "mp"),
    )
    return jax.shard_map(
        per_device, mesh=mesh, in_specs=in_specs, out_specs=out_specs, check_vma=False
    )
```

profile of v0, /device:TPU:0, one launch (start us, length us, event | category | flops | bytes accessed | tf_op | source)
XLA Modules:
  0.0 1162.6 jit_solution(9195493048433533163)
XLA Ops:
  10.9 34.9 %all-reduce.6 = (bf16[1024]{0:T(1024)(128)(2,1)S(1)}, bf16[1024]{0:T(1024)(128)(2,1)S(1)}) all-reduce(bf16[1024]{0:T(1024)(128)(2,1)S(1)} %dynamic-update-slice, bf16[1024]{0:T(1024)(128)(2,1)S(1)} %dynamic-update-slice.1), channel_id=1, replica_groups=mesh['dp'=16,'mp'=2] {'dp'}, use_global_device_ids=true, to_apply=%add | all-reduce | flops 2048 | bytes 8192
  54.3 19.5 %all-gather.13.cloned.1.call-done = bf16[2,320,1024]{2,1,0:T(8,128)(2,1)} async-done(((bf16[2,160,1024]{2,1,0:T(8,128)(2,1)}), bf16[2,320,1024]{2,1,0:T(8,128)(2,1)}) %all-gather.13.cloned.1.call-update) | async-done | bytes 1310736 | tf_op jit(solution)/shard_map/all_gather | solution.py:30
  73.8 47.4 %all-gather.15.cloned.1.call-done = bf16[1024,3,512]{2,0,1:T(8,128)(2,1)} async-done(((bf16[64,3,512]{2,0,1:T(8,128)(2,1)}), bf16[1024,3,512]{2,0,1:T(8,128)(2,1)}) %all-gather.15.cloned.1.call-update) | async-done | bytes 3145744 | tf_op jit(solution)/shard_map/all_gather | solution.py:140
  134.9 25.3 %all-gather.17.cloned.1.call-done = bf16[1024,512]{1,0:T(8,128)(2,1)} async-done(((bf16[64,512]{1,0:T(8,128)(2,1)}), bf16[1024,512]{1,0:T(8,128)(2,1)}) %all-gather.17.cloned.1.call-update) | async-done | bytes 1048592 | tf_op jit(solution)/shard_map/all_gather | solution.py:141
  164.7 20.1 %all-gather.25.cloned.1.call-done = bf16[2,320,1024]{2,1,0:T(8,128)(2,1)} async-done(((bf16[2,160,1024]{2,1,0:T(8,128)(2,1)}), bf16[2,320,1024]{2,1,0:T(8,128)(2,1)}) %all-gather.25.cloned.1.call-update) | async-done | bytes 1310736 | tf_op jit(solution)/shard_map/all_gather | solution.py:30
  202.1 23.0 %reduce-scatter.13.cloned.1.call-done = f32[2,160,1024]{2,1,0:T(8,128)} async-done(((f32[2,320,1024]{2,1,0:T(8,128)}), f32[2,160,1024]{2,1,0:T(8,128)}) %reduce-scatter.13.cloned.1.call-update) | async-done | bytes 1310736 | tf_op jit(solution)/shard_map/reduce_scatter | solution.py:34
  225.1 39.8 %reduce-scatter.17.cloned.1.call-done = f32[2,160,1024]{2,1,0:T(8,128)} async-done(((f32[2,320,1024]{2,1,0:T(8,128)}), f32[2,160,1024]{2,1,0:T(8,128)}) %reduce-scatter.17.cloned.1.call-update) | async-done | bytes 1310736 | tf_op jit(solution)/shard_map/reduce_scatter | solution.py:34
  270.9 46.7 %all-gather.21.cloned.1.call-done = bf16[1024,2048]{1,0:T(8,128)(2,1)} async-done(((bf16[64,2048]{1,0:T(8,128)(2,1)}), bf16[1024,2048]{1,0:T(8,128)(2,1)}) %all-gather.21.cloned.1.call-update) | async-done | bytes 4194320 | tf_op jit(solution)/shard_map/all_gather | solution.py:142
  317.6 24.9 %all-gather.19.cloned.1.call-done = bf16[2,320,1024]{2,1,0:T(8,128)(2,1)} async-done(((bf16[2,160,1024]{2,1,0:T(8,128)(2,1)}), bf16[2,320,1024]{2,1,0:T(8,128)(2,1)}) %all-gather.19.cloned.1.call-update) | async-done | bytes 1310736 | tf_op jit(solution)/shard_map/all_gather | solution.py:30
  342.5 6.9 fusion.107
  351.7 12.9 %multiply_convert_fusion.3 = (bf16[2,320,2048]{2,1,0:T(8,128)(2,1)}, f32[2,320,2048]{2,1,0:T(8,128)}) fusion(f32[2,320,2048]{2,1,0:T(8,128)S(1)} %get-tuple-element.87, u8[320,2048]{1,0:T(8,128)(4,1)S(1)} %get-tuple-element.10, u8[320,2048]{1,0:T(8,128)(4,1)S(1)} %get-tuple-element.9), kind=kLoop, calls=%fused_computation.47 | loop fusion | flops 91750400 | bytes 14417920 | tf_op jit(solution)/shard_map/convert_element_type | solution.py:167
  364.6 30.7 %all-gather.23.cloned.1.call-done = bf16[1024,2048]{1,0:T(8,128)(2,1)} async-done(((bf16[64,2048]{1,0:T(8,128)(2,1)}), bf16[1024,2048]{1,0:T(8,128)(2,1)}) %all-gather.23.cloned.1.call-update) | async-done | bytes 4194320 | tf_op jit(solution)/shard_map/all_gather | solution.py:143
  395.3 7.4 fusion.22
  402.9 16.5 %all-gather.27.cloned.1.call-done = bf16[2,320,1024]{2,1,0:T(8,128)(2,1)} async-done(((bf16[2,160,1024]{2,1,0:T(8,128)(2,1)}), bf16[2,320,1024]{2,1,0:T(8,128)(2,1)}) %all-gather.27.cloned.1.call-update) | async-done | bytes 1310736 | tf_op jit(solution)/shard_map/all_gather | solution.py:30
  419.5 6.9 fusion.108
  426.4 12.8 %multiply_convert_fusion.2 = (bf16[2,320,2048]{2,1,0:T(8,128)(2,1)S(1)}, f32[2,320,2048]{2,1,0:T(8,128)}) fusion(f32[2,320,2048]{2,1,0:T(8,128)S(1)} %get-tuple-element.86, u8[320,2048]{1,0:T(8,128)(4,1)S(1)} %get-tuple-element.12, u8[320,2048]{1,0:T(8,128)(4,1)S(1)} %get-tuple-element.11), kind=kLoop, calls=%fused_computation.34 | loop fusion | flops 91750400 | bytes 14417920 | tf_op jit(solution)/shard_map/convert_element_type | solution.py:167
  446.6 39.7 %psum.29 = f32[]{:T(128)} all-reduce(f32[]{:T(128)S(6)} %convert_element_type.181), channel_id=1, replica_groups=mesh['dp'=16,'mp'=2] {'dp','mp'}, use_global_device_ids=true, to_apply=%region_22.23 | all-reduce | flops 1 | bytes 8 | tf_op jit(solution)/shard_map/psum | solution.py:116
  487.1 13.4 %reduce-scatter.19.cloned.1.call-done = f32[2,160,1024]{2,1,0:T(8,128)} async-done(((f32[2,320,1024]{2,1,0:T(8,128)}), f32[2,160,1024]{2,1,0:T(8,128)}) %reduce-scatter.19.cloned.1.call-update) | async-done | bytes 1310736 | tf_op jit(solution)/shard_map/reduce_scatter | solution.py:34
  505.1 23.4 %all-gather.29.cloned.1.call-done = bf16[2,320,1024]{2,1,0:T(8,128)(2,1)} async-done(((bf16[2,160,1024]{2,1,0:T(8,128)(2,1)}), bf16[2,320,1024]{2,1,0:T(8,128)(2,1)}) %all-gather.29.cloned.1.call-update) | async-done | bytes 1310736 | tf_op jit(solution)/shard_map/all_gather | solution.py:38
  528.5 10.0 add_convert_fusion.1
  544.5 9.7 all-gather.33.cloned.1.call-done
  554.2 10.0 add_convert_fusion
  570.4 23.5 %reduce-scatter.21.cloned.1.call-done = f32[2,160,1024]{2,1,0:T(8,128)} async-done(((f32[2,320,1024]{2,1,0:T(8,128)}), f32[2,160,1024]{2,1,0:T(8,128)}) %reduce-scatter.21.cloned.1.call-update) | async-done | bytes 1310736 | tf_op jit(solution)/shard_map/reduce_scatter | solution.py:42
  593.9 39.8 %reduce-scatter.25.cloned.1.call-done = f32[2,160,1024]{2,1,0:T(8,128)} async-done(((f32[2,320,1024]{2,1,0:T(8,128)}), f32[2,160,1024]{2,1,0:T(8,128)}) %reduce-scatter.25.cloned.1.call-update) | async-done | bytes 1310736 | tf_op jit(solution)/shard_map/reduce_scatter | solution.py:42
  644.9 20.0 %all-gather.35.cloned.1.call-done = bf16[2,320,1024]{2,1,0:T(8,128)(2,1)} async-done(((bf16[2,160,1024]{2,1,0:T(8,128)(2,1)}), bf16[2,320,1024]{2,1,0:T(8,128)(2,1)}) %all-gather.35.cloned.1.call-update) | async-done | bytes 1310736 | tf_op jit(solution)/shard_map/all_gather | solution.py:38
  670.1 7.2 multiply_reduce_fusion
  729.0 6.3 fusion.60
  779.5 39.3 %psum.28 = f32[]{:T(128)} all-reduce(f32[]{:T(128)S(6)} %add.141), channel_id=1, replica_groups=mesh['dp'=16,'mp'=2] {'dp','mp'}, use_global_device_ids=true, to_apply=%region_20.21 | all-reduce | flops 1 | bytes 8 | tf_op jit(solution)/shard_map/psum | solution.py:235
  825.4 32.9 %all-reduce.4 = (f32[1024]{0:T(1024)S(1)}, f32[1024]{0:T(1024)S(1)}) all-reduce(f32[1024]{0:T(1024)S(1)} %add.148, f32[1024]{0:T(1024)S(1)} %add.151), channel_id=10, replica_groups=mesh['dp'=16,'mp'=2] {'dp'}, use_global_device_ids=true, to_apply=%region_39.40.clone | all-reduce | flops 2048 | bytes 16384
  868.5 86.4 %reduce-scatter.33.cloned.1.call-done = f32[64,2048]{1,0:T(8,128)} async-done(((f32[1024,2048]{1,0:T(8,128)}), f32[64,2048]{1,0:T(8,128)}) %reduce-scatter.33.cloned.1.call-update) | async-done | bytes 524304 | tf_op jit(solution)/shard_map/reduce_scatter | solution.py:231
  954.9 109.6 %reduce-scatter.35.cloned.1.call-done = f32[64,2048]{1,0:T(8,128)} async-done(((f32[1024,2048]{1,0:T(8,128)}), f32[64,2048]{1,0:T(8,128)}) %reduce-scatter.35.cloned.1.call-update) | async-done | bytes 524304 | tf_op jit(solution)/shard_map/reduce_scatter | solution.py:232
  1064.5 89.9 %reduce-scatter.29.cloned.1.call-done = f32[64,3,512]{2,0,1:T(8,128)} async-done(((f32[1024,3,512]{2,0,1:T(8,128)}), f32[64,3,512]{2,0,1:T(8,128)}) %reduce-scatter.29.cloned.1.call-update) | async-done | bytes 393232 | tf_op jit(solution)/shard_map/reduce_scatter | solution.py:229
  (284 shorter events, 203.7 us)
Async XLA Ops:
  7.2 47.1 %copy-start.47 = (s32[4,320]{1,0:T(4,128)S(1)}, s32[4,320]{1,0:T(4,128)}, u32[]{:S(2)}) copy-start(s32[4,320]{1,0:T(4,128)} %param.11) | copy-start | bytes 15364
  7.2 66.6 %all-gather.13.cloned.1.call-start = ((), (), s32[]{:S(2)}) async-start(), calls=%async_computation.12 | async-start | bytes 1966080 | tf_op jit(solution)/shard_map/all_gather | solution.py:30
  52.1 69.1 %all-gather.15.cloned.1.call-start = ((), (), s32[]{:S(2)}) async-start(), calls=%async_computation.13 | async-start | bytes 3342336 | tf_op jit(solution)/shard_map/all_gather | solution.py:140
  52.9 107.3 %all-gather.17.cloned.1.call-start = ((), (), s32[]{:S(2)}) async-start(), calls=%async_computation.14 | async-start | bytes 1114112 | tf_op jit(solution)/shard_map/all_gather | solution.py:141
  53.6 131.2 %all-gather.25.cloned.1.call-start = ((), (), s32[]{:S(2)}) async-start(), calls=%async_computation.20 | async-start | bytes 1966080 | tf_op jit(solution)/shard_map/all_gather | solution.py:30
  54.2 170.9 %reduce-scatter.13.cloned.1.call-start = ((), (), s32[]{:S(2)}) async-start(), calls=%async_computation.15 | async-start | bytes 3932160 | tf_op jit(solution)/shard_map/reduce_scatter | solution.py:34
  134.9 54.4 %copy-start.30 = (bf16[2,8,64,320]{3,2,1,0:T(8,128)(2,1)}, bf16[2,8,64,320]{3,2,1,0:T(8,128)(2,1)S(1)}, u32[]{:S(2)}) copy-start(bf16[2,8,64,320]{3,2,1,0:T(8,128)(2,1)S(1)} %fusion.79) | copy-start | bytes 1966084
  164.1 100.8 %reduce-scatter.17.cloned.1.call-start = ((), (), s32[]{:S(2)}) async-start(), calls=%async_computation.21 | async-start | bytes 3932160 | tf_op jit(solution)/shard_map/reduce_scatter | solution.py:34
  201.2 116.4 %all-gather.21.cloned.1.call-start = ((), (), s32[]{:S(2)}) async-start(), calls=%async_computation.17 | async-start | bytes 4456448 | tf_op jit(solution)/shard_map/all_gather | solution.py:142
  202.0 140.5 %all-gather.19.cloned.1.call-start = ((), (), s32[]{:S(2)}) async-start(), calls=%async_computation.16 | async-start | bytes 1966080 | tf_op jit(solution)/shard_map/all_gather | solution.py:30
  269.4 125.9 %all-gather.23.cloned.1.call-start = ((), (), s32[]{:S(2)}) async-start(), calls=%async_computation.18 | async-start | bytes 4456448 | tf_op jit(solution)/shard_map/all_gather | solution.py:143
  270.1 149.3 %all-gather.27.cloned.1.call-start = ((), (), s32[]{:S(2)}) async-start(), calls=%async_computation.22 | async-start | bytes 1966080 | tf_op jit(solution)/shard_map/all_gather | solution.py:30
  270.7 216.3 %reduce-scatter.15.cloned.1.call-start = ((), (), s32[]{:S(2)}) async-start(), calls=%async_computation.19 | async-start | bytes 3932160 | tf_op jit(solution)/shard_map/reduce_scatter | solution.py:34
  402.7 97.8 %reduce-scatter.19.cloned.1.call-start = ((), (), s32[]{:S(2)}) async-start(), calls=%async_computation.23 | async-start | bytes 3932160 | tf_op jit(solution)/shard_map/reduce_scatter | solution.py:34
  445.1 83.4 %all-gather.29.cloned.1.call-start = ((), (), s32[]{:S(2)}) async-start(), calls=%async_computation.24 | async-start | bytes 1966080 | tf_op jit(solution)/shard_map/all_gather | solution.py:38
  504.1 50.1 %all-gather.33.cloned.1.call-start = ((), (), s32[]{:S(2)}) async-start(), calls=%async_computation.28 | async-start | bytes 1966080 | tf_op jit(solution)/shard_map/all_gather | solution.py:38
  504.7 89.2 %reduce-scatter.21.cloned.1.call-start = ((), (), s32[]{:S(2)}) async-start(), calls=%async_computation.25 | async-start | bytes 3932160 | tf_op jit(solution)/shard_map/reduce_scatter | solution.py:42
  544.4 89.3 %reduce-scatter.25.cloned.1.call-start = ((), (), s32[]{:S(2)}) async-start(), calls=%async_computation.29 | async-start | bytes 3932160 | tf_op jit(solution)/shard_map/reduce_scatter | solution.py:42
  570.1 94.8 %all-gather.35.cloned.1.call-start = ((), (), s32[]{:S(2)}) async-start(), calls=%async_computation.30 | async-start | bytes 1966080 | tf_op jit(solution)/shard_map/all_gather | solution.py:38
  640.5 61.9 %all-gather.31.cloned.1.call-start = ((), (), s32[]{:S(2)}) async-start(), calls=%async_computation.26 | async-start | bytes 1966080 | tf_op jit(solution)/shard_map/all_gather | solution.py:38
  644.8 177.6 %reduce-scatter.27.cloned.1.call-start = ((), (), s32[]{:S(2)}) async-start(), calls=%async_computation.31 | async-start | bytes 3932160 | tf_op jit(solution)/shard_map/reduce_scatter | solution.py:42
  702.1 120.4 %reduce-scatter.23.cloned.1.call-start = ((), (), s32[]{:S(2)}) async-start(), calls=%async_computation.27 | async-start | bytes 3932160 | tf_op jit(solution)/shard_map/reduce_scatter | solution.py:42
  735.3 133.2 %reduce-scatter.31.cloned.1.call-start = ((), (), s32[]{:S(2)}) async-start(), calls=%async_computation.33 | async-start | bytes 2228224 | tf_op jit(solution)/shard_map/reduce_scatter | solution.py:230
  740.3 214.6 %reduce-scatter.33.cloned.1.call-start = ((), (), s32[]{:S(2)}) async-start(), calls=%async_computation.34 | async-start | bytes 8912896 | tf_op jit(solution)/shard_map/reduce_scatter | solution.py:231
  752.7 311.8 %reduce-scatter.35.cloned.1.call-start = ((), (), s32[]{:S(2)}) async-start(), calls=%async_computation.35 | async-start | bytes 8912896 | tf_op jit(solution)/shard_map/reduce_scatter | solution.py:232
  765.4 389.0 %reduce-scatter.29.cloned.1.call-start = ((), (), s32[]{:S(2)}) async-start(), calls=%async_computation.32 | async-start | bytes 6684672 | tf_op jit(solution)/shard_map/reduce_scatter | solution.py:229
  775.7 46.7 %copy-start.2 = (bf16[4,160,1024]{2,1,0:T(8,128)(2,1)S(1)}, bf16[4,160,1024]{2,1,0:T(8,128)(2,1)}, u32[]{:S(2)}) copy-start(bf16[4,160,1024]{2,1,0:T(8,128)(2,1)} %param.9) | copy-start | bytes 3932164
  775.8 46.7 %copy-start.42 = (f32[1024]{0:T(1024)S(1)}, f32[1024]{0:T(1024)}, u32[]{:S(2)}) copy-start(f32[1024]{0:T(1024)} %copy-done.41) | copy-start | bytes 12292
  775.8 46.7 %copy-start.44 = (f32[2,160]{1,0:T(2,128)S(1)}, f32[2,160]{1,0:T(2,128)}, u32[]{:S(2)}) copy-start(f32[2,160]{1,0:T(2,128)} %copy-done.43) | copy-start | bytes 3844
  775.8 46.7 %copy-start.46 = (f32[2,160]{1,0:T(2,128)S(1)}, f32[2,160]{1,0:T(2,128)}, u32[]{:S(2)}) copy-start(f32[2,160]{1,0:T(2,128)} %copy-done.45) | copy-start | bytes 3844
  775.8 46.7 %copy-start.49 = (f32[2,160]{1,0:T(2,128)S(1)}, f32[2,160]{1,0:T(2,128)}, u32[]{:S(2)}) copy-start(f32[2,160]{1,0:T(2,128)} %copy-done.48) | copy-start | bytes 3844
  775.8 88.0 %copy-start.15 = (f32[2,160,1024]{2,1,0:T(8,128)S(1)}, f32[2,160,1024]{2,1,0:T(8,128)}, u32[]{:S(2)}) copy-start(f32[2,160,1024]{2,1,0:T(8,128)} %get-tuple-element.45) | copy-start | bytes 3932164
  (58 other events, 446.8 us)
Sparse Core Ops, SparseCore 0:
  52.2 21.4 all-gather.12
  76.0 45.2 all-gather.14
  123.4 36.7 all-gather.16
  161.6 23.1 all-gather.24
  187.4 37.5 reduce-scatter.12
  227.2 37.5 reduce-scatter.16
  267.0 50.5 all-gather.20
  319.7 22.7 all-gather.18
  344.7 50.5 all-gather.22
  396.7 22.7 all-gather.26
  421.7 38.1 reduce-scatter.14
  462.0 38.3 reduce-scatter.18
  504.2 24.2 all-gather.28
  529.9 24.2 all-gather.32
  556.3 37.5 reduce-scatter.20
  596.1 37.5 reduce-scatter.24
  640.6 24.2 all-gather.34
  666.3 24.2 all-gather.30
  702.2 37.4 reduce-scatter.26
  741.9 37.5 reduce-scatter.22
  783.8 62.3 reduce-scatter.30
  851.4 103.5 reduce-scatter.32
  960.1 104.3 reduce-scatter.34
  1069.4 84.9 reduce-scatter.28
where the time goes:
time: 1170 us; the launch traced here: 1160 us
  waiting for transfers between devices  714 us (61%)
  matrix products  166 us (14%)
  blocking collectives  152 us (13%)
  other arithmetic  74.9 us (6%)
  local copies, waits for them, and re-layouts  30.3 us (3%)
  between operations  22.1 us (2%)
    reduce_scatter x1, waiting for transfers between devices, per_device(): lax.psum_scatter(summed[5], 'dp', scatter_dimension=0, tiled=True)  110 us
    reduce_scatter x1, waiting for transfers between devices, per_device(): lax.psum_scatter(summed[2], 'dp', scatter_dimension=0, tiled=True)  89.9 us
    reduce_scatter x1, waiting for transfers between devices, per_device(): lax.psum_scatter(summed[4], 'dp', scatter_dimension=0, tiled=True)  86.4 us
    all_gather x4, waiting for transfers between devices, full_rows(): return lax.all_gather(piece, 'mp', axis=1, tiled=True)  81 us
    reduce_scatter x4, waiting for transfers between devices, row_sums(): return lax.psum_scatter(partial_rows, 'mp', scatter_dimension=1, tiled=True)  76.2 us
    unnamed x2, blocking collectives  67.8 us
    reduce_scatter x4, waiting for transfers between devices, sum_grads(): return lax.psum_scatter(partial_rows, 'mp', scatter_dimension=1, tiled=True)  63.3 us
    all_gather x4, waiting for transfers between devices, full_grads(): return lax.all_gather(piece, 'mp', axis=1, tiled=True)  53.2 us
  transfers between devices with their start and end apart: 24, of which 19 were waited for; matrix products, arithmetic and copies ran while one was open for 20% of the time, Pallas kernels for 0%

commit v1 on v0

--- a/solution.py
+++ b/solution.py
@@ -113,7 +113,7 @@
     half_len = inputs.shape[1]
     offset = lax.axis_index("mp") * half_len
     keep_local = lax.dynamic_slice_in_dim(keep_mask, offset, half_len, 1)
-    valid_total = lax.psum(jnp.sum(keep_local).astype(jnp.float32), ("dp", "mp"))
+    valid_total = lax.psum(lax.psum(jnp.sum(keep_local).astype(jnp.float32), "mp"), "dp")
     token_total = inputs.shape[0] * lax.axis_size("dp") * half_len * lax.axis_size("mp")
     loss_factor = 2.0 * token_total / valid_total
     per_micro = inputs.shape[0] // MICRO

time: 1170 us -> 1170 us (level)
    psum x1 -> x2, blocking collectives: 39.7 us -> 38.5 us  [the longest x1 33 us: per_device(): lax.psum(lax.psum(jnp.sum(keep_local).astype(jnp.float32), 'mp'), 'dp')]
where the time goes in v1:
time: 1170 us; the launch traced here: 1160 us
  waiting for transfers between devices  715 us (61%)
  matrix products  165 us (14%)
  blocking collectives  151 us (13%)
  other arithmetic  74.9 us (6%)
  local copies, waits for them, and re-layouts  30.4 us (3%)
  between operations  22.1 us (2%)
    reduce_scatter x1, waiting for transfers between devices, per_device(): lax.psum_scatter(summed[5], 'dp', scatter_dimension=0, tiled=True)  110 us
    reduce_scatter x1, waiting for transfers between devices, per_device(): lax.psum_scatter(summed[2], 'dp', scatter_dimension=0, tiled=True)  89.9 us
    reduce_scatter x1, waiting for transfers between devices, per_device(): lax.psum_scatter(summed[4], 'dp', scatter_dimension=0, tiled=True)  86.6 us
    all_gather x4, waiting for transfers between devices, full_rows(): return lax.all_gather(piece, 'mp', axis=1, tiled=True)  81 us
    reduce_scatter x4, waiting for transfers between devices, row_sums(): return lax.psum_scatter(partial_rows, 'mp', scatter_dimension=1, tiled=True)  76.2 us
    unnamed x2, blocking collectives  67.8 us
    reduce_scatter x4, waiting for transfers between devices, sum_grads(): return lax.psum_scatter(partial_rows, 'mp', scatter_dimension=1, tiled=True)  63.3 us
    all_gather x4, waiting for transfers between devices, full_grads(): return lax.all_gather(piece, 'mp', axis=1, tiled=True)  53.1 us
  transfers between devices with their start and end apart: 24, of which 19 were waited for; matrix products, arithmetic and copies ran while one was open for 20% of the time, Pallas kernels for 0%

profile of v1, /device:TPU:0, one launch (start us, length us, event | category | flops | bytes accessed | tf_op | source)
XLA Modules:
  0.0 1161.6 jit_solution(548551790545562822)
XLA Ops:
  10.9 34.9 %all-reduce.6 = (bf16[1024]{0:T(1024)(128)(2,1)S(1)}, bf16[1024]{0:T(1024)(128)(2,1)S(1)}) all-reduce(bf16[1024]{0:T(1024)(128)(2,1)S(1)} %dynamic-update-slice, bf16[1024]{0:T(1024)(128)(2,1)S(1)} %dynamic-update-slice.1), channel_id=1, replica_groups=mesh['dp'=16,'mp'=2] {'dp'}, use_global_device_ids=true, to_apply=%add | all-reduce | flops 2048 | bytes 8192
  54.3 19.5 %all-gather.13.cloned.1.call-done = bf16[2,320,1024]{2,1,0:T(8,128)(2,1)} async-done(((bf16[2,160,1024]{2,1,0:T(8,128)(2,1)}), bf16[2,320,1024]{2,1,0:T(8,128)(2,1)}) %all-gather.13.cloned.1.call-update) | async-done | bytes 1310736 | tf_op jit(solution)/shard_map/all_gather | solution.py:30
  73.8 47.4 %all-gather.15.cloned.1.call-done = bf16[1024,3,512]{2,0,1:T(8,128)(2,1)} async-done(((bf16[64,3,512]{2,0,1:T(8,128)(2,1)}), bf16[1024,3,512]{2,0,1:T(8,128)(2,1)}) %all-gather.15.cloned.1.call-update) | async-done | bytes 3145744 | tf_op jit(solution)/shard_map/all_gather | solution.py:140
  134.9 25.3 %all-gather.17.cloned.1.call-done = bf16[1024,512]{1,0:T(8,128)(2,1)} async-done(((bf16[64,512]{1,0:T(8,128)(2,1)}), bf16[1024,512]{1,0:T(8,128)(2,1)}) %all-gather.17.cloned.1.call-update) | async-done | bytes 1048592 | tf_op jit(solution)/shard_map/all_gather | solution.py:141
  164.7 20.1 %all-gather.25.cloned.1.call-done = bf16[2,320,1024]{2,1,0:T(8,128)(2,1)} async-done(((bf16[2,160,1024]{2,1,0:T(8,128)(2,1)}), bf16[2,320,1024]{2,1,0:T(8,128)(2,1)}) %all-gather.25.cloned.1.call-update) | async-done | bytes 1310736 | tf_op jit(solution)/shard_map/all_gather | solution.py:30
  202.1 23.0 %reduce-scatter.13.cloned.1.call-done = f32[2,160,1024]{2,1,0:T(8,128)} async-done(((f32[2,320,1024]{2,1,0:T(8,128)}), f32[2,160,1024]{2,1,0:T(8,128)}) %reduce-scatter.13.cloned.1.call-update) | async-done | bytes 1310736 | tf_op jit(solution)/shard_map/reduce_scatter | solution.py:34
  225.1 39.8 %reduce-scatter.17.cloned.1.call-done = f32[2,160,1024]{2,1,0:T(8,128)} async-done(((f32[2,320,1024]{2,1,0:T(8,128)}), f32[2,160,1024]{2,1,0:T(8,128)}) %reduce-scatter.17.cloned.1.call-update) | async-done | bytes 1310736 | tf_op jit(solution)/shard_map/reduce_scatter | solution.py:34
  270.9 46.7 %all-gather.21.cloned.1.call-done = bf16[1024,2048]{1,0:T(8,128)(2,1)} async-done(((bf16[64,2048]{1,0:T(8,128)(2,1)}), bf16[1024,2048]{1,0:T(8,128)(2,1)}) %all-gather.21.cloned.1.call-update) | async-done | bytes 4194320 | tf_op jit(solution)/shard_map/all_gather | solution.py:142
  317.6 24.9 %all-gather.19.cloned.1.call-done = bf16[2,320,1024]{2,1,0:T(8,128)(2,1)} async-done(((bf16[2,160,1024]{2,1,0:T(8,128)(2,1)}), bf16[2,320,1024]{2,1,0:T(8,128)(2,1)}) %all-gather.19.cloned.1.call-update) | async-done | bytes 1310736 | tf_op jit(solution)/shard_map/all_gather | solution.py:30
  342.5 6.9 fusion.107
  351.7 12.9 %multiply_convert_fusion.3 = (bf16[2,320,2048]{2,1,0:T(8,128)(2,1)}, f32[2,320,2048]{2,1,0:T(8,128)}) fusion(f32[2,320,2048]{2,1,0:T(8,128)S(1)} %get-tuple-element.87, u8[320,2048]{1,0:T(8,128)(4,1)S(1)} %get-tuple-element.10, u8[320,2048]{1,0:T(8,128)(4,1)S(1)} %get-tuple-element.9), kind=kLoop, calls=%fused_computation.47 | loop fusion | flops 91750400 | bytes 14417920 | tf_op jit(solution)/shard_map/convert_element_type | solution.py:167
  364.6 30.7 %all-gather.23.cloned.1.call-done = bf16[1024,2048]{1,0:T(8,128)(2,1)} async-done(((bf16[64,2048]{1,0:T(8,128)(2,1)}), bf16[1024,2048]{1,0:T(8,128)(2,1)}) %all-gather.23.cloned.1.call-update) | async-done | bytes 4194320 | tf_op jit(solution)/shard_map/all_gather | solution.py:143
  395.3 7.4 fusion.22
  402.9 16.5 %all-gather.27.cloned.1.call-done = bf16[2,320,1024]{2,1,0:T(8,128)(2,1)} async-done(((bf16[2,160,1024]{2,1,0:T(8,128)(2,1)}), bf16[2,320,1024]{2,1,0:T(8,128)(2,1)}) %all-gather.27.cloned.1.call-update) | async-done | bytes 1310736 | tf_op jit(solution)/shard_map/all_gather | solution.py:30
  419.5 6.9 fusion.108
  426.4 12.8 %multiply_convert_fusion.2 = (bf16[2,320,2048]{2,1,0:T(8,128)(2,1)S(1)}, f32[2,320,2048]{2,1,0:T(8,128)}) fusion(f32[2,320,2048]{2,1,0:T(8,128)S(1)} %get-tuple-element.86, u8[320,2048]{1,0:T(8,128)(4,1)S(1)} %get-tuple-element.12, u8[320,2048]{1,0:T(8,128)(4,1)S(1)} %get-tuple-element.11), kind=kLoop, calls=%fused_computation.34 | loop fusion | flops 91750400 | bytes 14417920 | tf_op jit(solution)/shard_map/convert_element_type | solution.py:167
  452.0 33.0 %psum.37 = f32[]{:T(128)} all-reduce(f32[]{:T(128)} %psum.36), channel_id=1, replica_groups=mesh['dp'=16,'mp'=2] {'dp'}, use_global_device_ids=true, to_apply=%region_23.24 | all-reduce | flops 1 | bytes 8 | tf_op jit(solution)/shard_map/psum | solution.py:116
  485.8 13.4 %reduce-scatter.19.cloned.1.call-done = f32[2,160,1024]{2,1,0:T(8,128)} async-done(((f32[2,320,1024]{2,1,0:T(8,128)}), f32[2,160,1024]{2,1,0:T(8,128)}) %reduce-scatter.19.cloned.1.call-update) | async-done | bytes 1310736 | tf_op jit(solution)/shard_map/reduce_scatter | solution.py:34
  503.9 23.4 %all-gather.29.cloned.1.call-done = bf16[2,320,1024]{2,1,0:T(8,128)(2,1)} async-done(((bf16[2,160,1024]{2,1,0:T(8,128)(2,1)}), bf16[2,320,1024]{2,1,0:T(8,128)(2,1)}) %all-gather.29.cloned.1.call-update) | async-done | bytes 1310736 | tf_op jit(solution)/shard_map/all_gather | solution.py:38
  527.3 10.0 add_convert_fusion.1
  543.3 9.7 all-gather.33.cloned.1.call-done
  553.0 10.0 add_convert_fusion
  569.1 23.5 %reduce-scatter.21.cloned.1.call-done = f32[2,160,1024]{2,1,0:T(8,128)} async-done(((f32[2,320,1024]{2,1,0:T(8,128)}), f32[2,160,1024]{2,1,0:T(8,128)}) %reduce-scatter.21.cloned.1.call-update) | async-done | bytes 1310736 | tf_op jit(solution)/shard_map/reduce_scatter | solution.py:42
  592.7 39.8 %reduce-scatter.25.cloned.1.call-done = f32[2,160,1024]{2,1,0:T(8,128)} async-done(((f32[2,320,1024]{2,1,0:T(8,128)}), f32[2,160,1024]{2,1,0:T(8,128)}) %reduce-scatter.25.cloned.1.call-update) | async-done | bytes 1310736 | tf_op jit(solution)/shard_map/reduce_scatter | solution.py:42
  643.6 20.1 %all-gather.35.cloned.1.call-done = bf16[2,320,1024]{2,1,0:T(8,128)(2,1)} async-done(((bf16[2,160,1024]{2,1,0:T(8,128)(2,1)}), bf16[2,320,1024]{2,1,0:T(8,128)(2,1)}) %all-gather.35.cloned.1.call-update) | async-done | bytes 1310736 | tf_op jit(solution)/shard_map/all_gather | solution.py:38
  668.9 7.2 multiply_reduce_fusion
  727.9 6.3 fusion.60
  778.3 39.3 %psum.35 = f32[]{:T(128)} all-reduce(f32[]{:T(128)S(6)} %add.143), channel_id=1, replica_groups=mesh['dp'=16,'mp'=2] {'dp','mp'}, use_global_device_ids=true, to_apply=%region_20.21 | all-reduce | flops 1 | bytes 8 | tf_op jit(solution)/shard_map/psum | solution.py:235
  824.1 32.9 %all-reduce.4 = (f32[1024]{0:T(1024)S(1)}, f32[1024]{0:T(1024)S(1)}) all-reduce(f32[1024]{0:T(1024)S(1)} %add.150, f32[1024]{0:T(1024)S(1)} %add.153), channel_id=10, replica_groups=mesh['dp'=16,'mp'=2] {'dp'}, use_global_device_ids=true, to_apply=%region_40.41.clone | all-reduce | flops 2048 | bytes 16384
  867.3 86.6 %reduce-scatter.33.cloned.1.call-done = f32[64,2048]{1,0:T(8,128)} async-done(((f32[1024,2048]{1,0:T(8,128)}), f32[64,2048]{1,0:T(8,128)}) %reduce-scatter.33.cloned.1.call-update) | async-done | bytes 524304 | tf_op jit(solution)/shard_map/reduce_scatter | solution.py:231
  953.9 109.6 %reduce-scatter.35.cloned.1.call-done = f32[64,2048]{1,0:T(8,128)} async-done(((f32[1024,2048]{1,0:T(8,128)}), f32[64,2048]{1,0:T(8,128)}) %reduce-scatter.35.cloned.1.call-update) | async-done | bytes 524304 | tf_op jit(solution)/shard_map/reduce_scatter | solution.py:232
  1063.5 89.9 %reduce-scatter.29.cloned.1.call-done = f32[64,3,512]{2,0,1:T(8,128)} async-done(((f32[1024,3,512]{2,0,1:T(8,128)}), f32[64,3,512]{2,0,1:T(8,128)}) %reduce-scatter.29.cloned.1.call-update) | async-done | bytes 393232 | tf_op jit(solution)/shard_map/reduce_scatter | solution.py:229
  (285 shorter events, 209.2 us)
Async XLA Ops:
  7.2 47.1 %copy-start.47 = (s32[4,320]{1,0:T(4,128)S(1)}, s32[4,320]{1,0:T(4,128)}, u32[]{:S(2)}) copy-start(s32[4,320]{1,0:T(4,128)} %param.11) | copy-start | bytes 15364
  7.2 66.6 %all-gather.13.cloned.1.call-start = ((), (), s32[]{:S(2)}) async-start(), calls=%async_computation.12 | async-start | bytes 1966080 | tf_op jit(solution)/shard_map/all_gather | solution.py:30
  52.1 69.1 %all-gather.15.cloned.1.call-start = ((), (), s32[]{:S(2)}) async-start(), calls=%async_computation.13 | async-start | bytes 3342336 | tf_op jit(solution)/shard_map/all_gather | solution.py:140
  52.9 107.3 %all-gather.17.cloned.1.call-start = ((), (), s32[]{:S(2)}) async-start(), calls=%async_computation.14 | async-start | bytes 1114112 | tf_op jit(solution)/shard_map/all_gather | solution.py:141
  53.6 131.2 %all-gather.25.cloned.1.call-start = ((), (), s32[]{:S(2)}) async-start(), calls=%async_computation.20 | async-start | bytes 1966080 | tf_op jit(solution)/shard_map/all_gather | solution.py:30
  54.2 170.9 %reduce-scatter.13.cloned.1.call-start = ((), (), s32[]{:S(2)}) async-start(), calls=%async_computation.15 | async-start | bytes 3932160 | tf_op jit(solution)/shard_map/reduce_scatter | solution.py:34
  134.9 54.4 %copy-start.30 = (bf16[2,8,64,320]{3,2,1,0:T(8,128)(2,1)}, bf16[2,8,64,320]{3,2,1,0:T(8,128)(2,1)S(1)}, u32[]{:S(2)}) copy-start(bf16[2,8,64,320]{3,2,1,0:T(8,128)(2,1)S(1)} %fusion.79) | copy-start | bytes 1966084
  164.1 100.8 %reduce-scatter.17.cloned.1.call-start = ((), (), s32[]{:S(2)}) async-start(), calls=%async_computation.21 | async-start | bytes 3932160 | tf_op jit(solution)/shard_map/reduce_scatter | solution.py:34
  201.2 116.4 %all-gather.21.cloned.1.call-start = ((), (), s32[]{:S(2)}) async-start(), calls=%async_computation.17 | async-start | bytes 4456448 | tf_op jit(solution)/shard_map/all_gather | solution.py:142
  202.0 140.5 %all-gather.19.cloned.1.call-start = ((), (), s32[]{:S(2)}) async-start(), calls=%async_computation.16 | async-start | bytes 1966080 | tf_op jit(solution)/shard_map/all_gather | solution.py:30
  269.4 125.9 %all-gather.23.cloned.1.call-start = ((), (), s32[]{:S(2)}) async-start(), calls=%async_computation.18 | async-start | bytes 4456448 | tf_op jit(solution)/shard_map/all_gather | solution.py:143
  270.1 149.3 %all-gather.27.cloned.1.call-start = ((), (), s32[]{:S(2)}) async-start(), calls=%async_computation.22 | async-start | bytes 1966080 | tf_op jit(solution)/shard_map/all_gather | solution.py:30
  270.7 215.1 %reduce-scatter.15.cloned.1.call-start = ((), (), s32[]{:S(2)}) async-start(), calls=%async_computation.19 | async-start | bytes 3932160 | tf_op jit(solution)/shard_map/reduce_scatter | solution.py:34
  402.7 96.5 %reduce-scatter.19.cloned.1.call-start = ((), (), s32[]{:S(2)}) async-start(), calls=%async_computation.23 | async-start | bytes 3932160 | tf_op jit(solution)/shard_map/reduce_scatter | solution.py:34
  445.1 82.2 %all-gather.29.cloned.1.call-start = ((), (), s32[]{:S(2)}) async-start(), calls=%async_computation.24 | async-start | bytes 1966080 | tf_op jit(solution)/shard_map/all_gather | solution.py:38
  502.9 50.1 %all-gather.33.cloned.1.call-start = ((), (), s32[]{:S(2)}) async-start(), calls=%async_computation.28 | async-start | bytes 1966080 | tf_op jit(solution)/shard_map/all_gather | solution.py:38
  503.4 89.2 %reduce-scatter.21.cloned.1.call-start = ((), (), s32[]{:S(2)}) async-start(), calls=%async_computation.25 | async-start | bytes 3932160 | tf_op jit(solution)/shard_map/reduce_scatter | solution.py:42
  543.2 89.2 %reduce-scatter.25.cloned.1.call-start = ((), (), s32[]{:S(2)}) async-start(), calls=%async_computation.29 | async-start | bytes 3932160 | tf_op jit(solution)/shard_map/reduce_scatter | solution.py:42
  568.9 94.8 %all-gather.35.cloned.1.call-start = ((), (), s32[]{:S(2)}) async-start(), calls=%async_computation.30 | async-start | bytes 1966080 | tf_op jit(solution)/shard_map/all_gather | solution.py:38
  639.3 62.0 %all-gather.31.cloned.1.call-start = ((), (), s32[]{:S(2)}) async-start(), calls=%async_computation.26 | async-start | bytes 1966080 | tf_op jit(solution)/shard_map/all_gather | solution.py:38
  643.6 177.6 %reduce-scatter.27.cloned.1.call-start = ((), (), s32[]{:S(2)}) async-start(), calls=%async_computation.31 | async-start | bytes 3932160 | tf_op jit(solution)/shard_map/reduce_scatter | solution.py:42
  701.0 120.2 %reduce-scatter.23.cloned.1.call-start = ((), (), s32[]{:S(2)}) async-start(), calls=%async_computation.27 | async-start | bytes 3932160 | tf_op jit(solution)/shard_map/reduce_scatter | solution.py:42
  734.3 133.0 %reduce-scatter.31.cloned.1.call-start = ((), (), s32[]{:S(2)}) async-start(), calls=%async_computation.33 | async-start | bytes 2228224 | tf_op jit(solution)/shard_map/reduce_scatter | solution.py:230
  739.2 214.7 %reduce-scatter.33.cloned.1.call-start = ((), (), s32[]{:S(2)}) async-start(), calls=%async_computation.34 | async-start | bytes 8912896 | tf_op jit(solution)/shard_map/reduce_scatter | solution.py:231
  751.5 312.0 %reduce-scatter.35.cloned.1.call-start = ((), (), s32[]{:S(2)}) async-start(), calls=%async_computation.35 | async-start | bytes 8912896 | tf_op jit(solution)/shard_map/reduce_scatter | solution.py:232
  764.1 389.3 %reduce-scatter.29.cloned.1.call-start = ((), (), s32[]{:S(2)}) async-start(), calls=%async_computation.32 | async-start | bytes 6684672 | tf_op jit(solution)/shard_map/reduce_scatter | solution.py:229
  774.5 46.7 %copy-start.2 = (bf16[4,160,1024]{2,1,0:T(8,128)(2,1)S(1)}, bf16[4,160,1024]{2,1,0:T(8,128)(2,1)}, u32[]{:S(2)}) copy-start(bf16[4,160,1024]{2,1,0:T(8,128)(2,1)} %param.9) | copy-start | bytes 3932164
  774.5 46.7 %copy-start.42 = (f32[1024]{0:T(1024)S(1)}, f32[1024]{0:T(1024)}, u32[]{:S(2)}) copy-start(f32[1024]{0:T(1024)} %copy-done.41) | copy-start | bytes 12292
  774.5 46.7 %copy-start.44 = (f32[2,160]{1,0:T(2,128)S(1)}, f32[2,160]{1,0:T(2,128)}, u32[]{:S(2)}) copy-start(f32[2,160]{1,0:T(2,128)} %copy-done.43) | copy-start | bytes 3844
  774.5 46.7 %copy-start.46 = (f32[2,160]{1,0:T(2,128)S(1)}, f32[2,160]{1,0:T(2,128)}, u32[]{:S(2)}) copy-start(f32[2,160]{1,0:T(2,128)} %copy-done.45) | copy-start | bytes 3844
  774.5 46.7 %copy-start.49 = (f32[2,160]{1,0:T(2,128)S(1)}, f32[2,160]{1,0:T(2,128)}, u32[]{:S(2)}) copy-start(f32[2,160]{1,0:T(2,128)} %copy-done.48) | copy-start | bytes 3844
  774.6 88.0 %copy-start.15 = (f32[2,160,1024]{2,1,0:T(8,128)S(1)}, f32[2,160,1024]{2,1,0:T(8,128)}, u32[]{:S(2)}) copy-start(f32[2,160,1024]{2,1,0:T(8,128)} %get-tuple-element.45) | copy-start | bytes 3932164
  (58 other events, 447.1 us)
Sparse Core Ops, SparseCore 0:
  52.2 21.4 all-gather.12
  76.0 45.2 all-gather.14
  123.4 36.7 all-gather.16
  161.6 23.1 all-gather.24
  187.4 37.5 reduce-scatter.12
  227.2 37.5 reduce-scatter.16
  267.0 50.5 all-gather.20
  319.7 22.7 all-gather.18
  344.7 50.5 all-gather.22
  396.7 22.7 all-gather.26
  421.7 37.6 reduce-scatter.14
  461.6 37.5 reduce-scatter.18
  503.0 24.2 all-gather.28
  528.7 24.2 all-gather.32
  555.1 37.5 reduce-scatter.20
  594.9 37.5 reduce-scatter.24
  639.4 24.2 all-gather.34
  665.1 24.2 all-gather.30
  701.1 37.4 reduce-scatter.26
  740.8 37.5 reduce-scatter.22
  782.8 62.1 reduce-scatter.30
  850.2 103.6 reduce-scatter.32
  959.1 104.4 reduce-scatter.34
  1068.4 84.9 reduce-scatter.28
